TPU v7x, 128 devices: a whole 4x4x4 slice. The times are simulated.
128 devices in a mesh: section: 4 (over z), space: 32 (over x, y, core).
Axes of the slice: x: 4, y: 4, z: 4, core: 2. Of those that a mesh axis runs over, the one named last changes fastest.
Arguments:
- features: bfloat16 [4, 128, 784, 256], P('section', 'space')
- tissue: int32 [4, 128], P('section'), may hold values from 0 to 1, as said below
- first_weight: bfloat16 [256, 512], replicated, may hold values from -0.375 to 0.375
- first_gain: float32 [512], replicated, may hold values from 0.1 to 1.9
- first_bias: float32 [512], replicated, may hold values from -3 to 3
- second_weight: bfloat16 [512, 1024], P(None, 'space'), may hold values from -0.25 to 0.25
- second_gain: float32 [1024], replicated, may hold values from 0.1 to 1.9
- second_bias: float32 [1024], replicated, may hold values from -3 to 3
Outputs:
- output: bfloat16 [4, 1024, 100352], P('section', 'space')
- first_mean: float32 [512], replicated
- first_var: float32 [512], replicated
- second_mean: float32 [1024], P('space')
- second_var: float32 [1024], P('space')
Inputs may be any that keep to these rules, and one draw needn't show every extreme that they name: Every tile row holds at least one tissue tile and at least one tile without tissue.
All inputs are finite; a program needn't handle non-finite values.
Results may differ from a plain program's by a relative error of at most 0.0053.
Values may be sent and summed in bfloat16 or wider, within the bound.
No kernel may reach another device: no remote copies, remote signals or barrier semaphores. Data moves between devices by JAX's collectives and lax.ppermute only.
A program may use at most 128 MiB of HBM per device.

v0:
```python
import jax
import jax.numpy as jnp
from jax import lax
from jax.sharding import PartitionSpec as P

EPS = 1e-05


def normalize(values, mean_val, var_val, gain, bias):
    return jnp.maximum(gain * (values - mean_val) * lax.rsqrt(var_val + EPS) + bias, 0.0)


def masked_sum(values, weight):
    return jnp.sum(values * weight, axis=(0, 1, 2))


def masked_squares(values, weight, mean_val):
    centred = values - mean_val
    return jnp.sum(weight * centred * centred, axis=(0, 1, 2))


def channel_first(values):
    batch, tiles_here, pixels, chans = values.shape
    return jnp.transpose(values, (0, 3, 1, 2)).reshape(batch, chans, tiles_here * pixels)


def shards(
    features, tissue, first_weight, first_gain, first_bias, second_weight, second_gain, second_bias
):
    index = lax.axis_index("space")
    tiles_here = features.shape[1]
    pixels = features.shape[2]
    row_mask = tissue[0].astype(jnp.float32)
    own_mask = lax.dynamic_slice_in_dim(row_mask, index * tiles_here, tiles_here)
    own_weight = own_mask[None, :, None, None]
    local_count = jnp.sum(own_mask) * pixels
    first = jnp.einsum("mtpc,cd->mtpd", features, first_weight, preferred_element_type=jnp.float32)
    total, count = lax.psum((masked_sum(first, own_weight), local_count), ("section", "space"))
    first_mean = total / count
    first_var = (
        lax.psum(masked_squares(first, own_weight, first_mean), ("section", "space")) / count
    )
    activation = normalize(first, first_mean, first_var, first_gain, first_bias).astype(
        jnp.bfloat16
    )
    second = jnp.einsum(
        "mtpc,cd->mtpd",
        activation,
        lax.all_gather(second_weight, "space", axis=1, tiled=True),
        preferred_element_type=jnp.float32,
    )
    width_here = second_weight.shape[1]
    moved = lax.all_to_all(channel_first(second), "space", split_axis=1, concat_axis=2, tiled=True)
    row_weight = jnp.repeat(row_mask, pixels)[None, None, :]
    second_mean = lax.psum(jnp.sum(moved * row_weight, axis=(0, 2)), "section") / count
    centred = moved - second_mean[:, None]
    second_var = lax.psum(jnp.sum(row_weight * centred * centred, axis=(0, 2)), "section") / count
    gain_here = lax.dynamic_slice_in_dim(second_gain, index * width_here, width_here)
    bias_here = lax.dynamic_slice_in_dim(second_bias, index * width_here, width_here)
    output = normalize(
        moved, second_mean[:, None], second_var[:, None], gain_here[:, None], bias_here[:, None]
    ).astype(jnp.bfloat16)
    return (output, first_mean, first_var, second_mean, second_var)


def solution(mesh):
    in_specs = (
        P("section", "space", None, None),
        P("section", None),
        P(),
        P(),
        P(),
        P(None, "space"),
        P(),
        P(),
    )
    out_specs = (P("section", "space", None), P(), P(), P("space"), P("space"))
    return jax.shard_map(shards, mesh=mesh, in_specs=in_specs, out_specs=out_specs, check_vma=False)
```

profile of v0, /device:TPU:44, one launch (start us, length us, event | category | flops | bytes accessed | tf_op | source)
XLA Modules:
  0.0 490.6 jit_solution(13047732161503273822)
XLA Ops:
  7.2 0.7 all-gather.2.cloned.1.call-update
  8.6 0.7 fusion.12
  9.9 4.7 multiply_reduce_fusion.1
  14.6 64.0 %all-reduce = (f32[512]{0:T(512)S(1)}, f32[]{:T(128)}) all-reduce(f32[512]{0:T(512)S(1)} %get-tuple-element.13, f32[]{:T(128)S(6)} %mul.112), channel_id=1, replica_groups=mesh['section'=4,'space'=32] {'section','space'}, use_global_device_ids=true, to_apply=%region_1.0 | all-reduce | flops 513 | bytes 4104 | tf_op jit(solution)/shard_map/psum | solution.py:38
  78.6 0.7 broadcast_divide_fusion.1
  79.3 3.9 fusion.1
  83.2 62.5 %psum.37 = f32[512]{0:T(512)S(1)} all-reduce(f32[512]{0:T(512)S(1)} %fusion.1), channel_id=1, replica_groups=mesh['section'=4,'space'=32] {'section','space'}, use_global_device_ids=true, to_apply=%region_5.0 | all-reduce | flops 512 | bytes 4096 | tf_op jit(solution)/shard_map/psum | solution.py:41
  145.7 1.3 add_rsqrt_fusion
  147.0 11.2 %fusion.2 = f32[4,784,1024]{2,1,0:T(8,128)} fusion(f32[4,784,512]{2,1,0:T(8,128)} %get-tuple-element.14, f32[512]{0:T(512)S(1)} %copy-done.4, f32[512]{0:T(512)S(1)} %get-tuple-element.9, f32[512]{0:T(512)S(1)} %broadcast_divide_fusion.1, f32[512]{0:T(512)S(1)} %copy-done.5, bf16[512,1024]{0,1:T(8,128)(2,1)} %all-gather.2.cloned.1.call-done), kind=kOutput, calls=%fused_computation.8 | convolution fusion | flops 3297968128 | bytes 20324352 | tf_op jit(solution)/shard_map/mtpc,cd->mtpd/dot_general | solution.py:46
  158.2 27.1 %copy.17 = f32[1,1024,3136]{2,0,1:T(1,128)} copy(f32[1,1024,3136]{1,2,0:T(8,128)} %bitcast.28) | data formatting | bytes 25690112 | tf_op jit(solution)/shard_map/reshape | solution.py:24
  185.3 8.8 %all-to-all-start = ((f32[1,1024,3136]{2,0,1:T(1,128)}), f32[1,1024,3136]{2,0,1:T(1,128)}, u32[]{:S(2)}, u32[]{:S(2)}) async-start(f32[1,1024,3136]{2,0,1:T(1,128)} %copy.17), calls=%async_computation | async-start | bytes 26214400 | tf_op jit(solution)/shard_map/all_to_all | solution.py:53
  194.6 0.8 dynamic_slice.11
  195.4 0.8 dynamic_slice.14
  196.2 204.3 %all-to-all-done = f32[1,1024,3136]{2,0,1:T(1,128)} async-done(((f32[1,1024,3136]{2,0,1:T(1,128)}), f32[1,1024,3136]{2,0,1:T(1,128)}, u32[]{:S(2)}, u32[]{:S(2)}) %all-to-all-start) | async-done | bytes 12845088 | tf_op jit(solution)/shard_map/all_to_all | solution.py:53
  400.4 10.3 %copy.19 = f32[1,1024,3136]{2,1,0:T(8,128)} copy(f32[1,1024,3136]{2,0,1:T(1,128)} %all-to-all-done) | data formatting | bytes 25690112
  410.7 17.0 %copy.18 = f32[1,32,32,3136]{3,2,1,0:T(8,128)} copy(f32[1,32,32,3136]{3,1,2,0:T(8,128)} %bitcast.25) | data formatting | bytes 25690112 | tf_op jit(solution)/shard_map/all_to_all | solution.py:53
  427.7 5.7 %multiply_reduce_fusion = f32[32]{0:T(128)S(1)} fusion(f32[1,32,32,3136]{3,1,2,0:T(8,128)} %bitcast.26, f32[32,3136]{1,0:T(8,128)S(1)} %broadcast_in_dim.5), kind=kLoop, calls=%fused_computation.2 | loop fusion | flops 6422496 | bytes 13246592 | tf_op jit(solution)/shard_map/reduce_sum | solution.py:55
  433.4 9.0 %psum.38 = f32[32]{0:T(128)S(1)} all-reduce(f32[32]{0:T(128)S(1)} %multiply_reduce_fusion), channel_id=1, replica_groups=mesh['section'=4,'space'=32] {'section'}, use_global_device_ids=true, to_apply=%region_7.0 | all-reduce | flops 32 | bytes 256 | tf_op jit(solution)/shard_map/psum | solution.py:55
  442.4 0.7 broadcast_divide_fusion.3
  443.1 6.6 %fusion = f32[32]{0:T(128)S(1)} fusion(f32[1,32,32,3136]{3,1,2,0:T(8,128)} %bitcast.27, f32[32]{0:T(128)S(1)} %broadcast_divide_fusion.3, f32[32,3136]{1,0:T(8,128)S(1)} %broadcast_in_dim.5), kind=kLoop, calls=%fused_computation.1 | loop fusion | flops 12845024 | bytes 13246720 | tf_op jit(solution)/shard_map/reduce_sum | solution.py:57
  449.7 9.9 %psum.39 = f32[32]{0:T(128)S(1)} all-reduce(f32[32]{0:T(128)S(1)} %fusion), channel_id=1, replica_groups=mesh['section'=4,'space'=32] {'section'}, use_global_device_ids=true, to_apply=%region_9.0 | all-reduce | flops 32 | bytes 256 | tf_op jit(solution)/shard_map/psum | solution.py:57
  459.6 1.2 add_rsqrt_fusion.1
  460.8 12.9 %all_to_all.16 = f32[1,32,100352]{2,1,0:T(8,128)} reshape(f32[1,32,32,3136]{3,2,1,0:T(8,128)} %copy.18) | data formatting | bytes 25690112 | tf_op jit(solution)/shard_map/all_to_all | solution.py:53
  473.7 10.0 %maximum_convert_fusion = bf16[1,32,100352]{2,1,0:T(8,128)(2,1)} fusion(f32[1,32,100352]{2,1,0:T(8,128)} %all_to_all.16, f32[32]{0:T(128)S(1)} %dynamic_slice.14, f32[32]{0:T(128)S(1)} %get-tuple-element.7, f32[32]{0:T(128)S(1)} %broadcast_divide_fusion.3, f32[32]{0:T(128)S(1)} %dynamic_slice.11), kind=kLoop, calls=%fused_computation.3 | loop fusion | flops 19267584 | bytes 19268096 | tf_op jit(solution)/shard_map/convert_element_type | solution.py:62
  (21 shorter events, 1.2 us)
Async XLA Ops:
  7.2 2.7 copy-start
  7.2 139.8 %all-gather.2.cloned.1.call-start = ((), (), s32[]{:S(2)}) async-start(), calls=%async_computation.1 | async-start | bytes 1081344 | tf_op jit(solution)/shard_map/all_gather | solution.py:49
  14.6 132.3 %copy-start.4 = (f32[512]{0:T(512)S(1)}, f32[512]{0:T(512)}, u32[]{:S(2)}) copy-start(f32[512]{0:T(512)} %param.12) | copy-start | bytes 6148
  14.6 132.4 %copy-start.5 = (f32[512]{0:T(512)S(1)}, f32[512]{0:T(512)}, u32[]{:S(2)}) copy-start(f32[512]{0:T(512)} %param.11) | copy-start | bytes 6148
  79.3 78.9 %copy-start.2 = (f32[512]{0:T(512)}, f32[512]{0:T(512)S(1)}, u32[]{:S(2)}) copy-start(f32[512]{0:T(512)S(1)} %broadcast_divide_fusion.1) | copy-start | bytes 6148
  185.3 8.8 %copy-start.6 = (s32[1,128]{1,0:T(1,128)S(1)}, s32[1,128]{1,0:T(1,128)}, u32[]{:S(2)}) copy-start(s32[1,128]{1,0:T(1,128)} %param.9) | copy-start | bytes 1540
  185.3 215.1 %all-to-all-start = ((f32[1,1024,3136]{2,0,1:T(1,128)}), f32[1,1024,3136]{2,0,1:T(1,128)}, u32[]{:S(2)}, u32[]{:S(2)}) async-start(f32[1,1024,3136]{2,0,1:T(1,128)} %copy.17), calls=%async_computation | async-start | bytes 26214400 | tf_op jit(solution)/shard_map/all_to_all | solution.py:53
  443.1 30.7 %copy-start.3 = (f32[32]{0:T(128)}, f32[32]{0:T(128)S(1)}, u32[]{:S(2)}) copy-start(f32[32]{0:T(128)S(1)} %broadcast_divide_fusion.3) | copy-start | bytes 388
  473.7 10.0 %copy-start.1 = (bf16[1,4,784,256]{3,2,1,0:T(8,128)(2,1)S(1)}, bf16[1,4,784,256]{3,2,1,0:T(8,128)(2,1)}, u32[]{:S(2)}) copy-start(bf16[1,4,784,256]{3,2,1,0:T(8,128)(2,1)} %param.8) | copy-start | bytes 4816900
Sparse Core Ops, SparseCore 0:
  10.3 42.4 all-gather.1
where the time goes:
time: 492 us; the launch traced here: 491 us
  waiting for transfers between devices  205 us (42%)
  blocking collectives  145 us (29%)
  local copies, waits for them, and re-layouts  69.3 us (14%)
  other arithmetic  31.4 us (6%)
  matrix products  15.9 us (3%)
  between operations  14.8 us (3%)
  starting transfers between devices  8.84 us (2%)
    all_to_all x1, waiting for transfers between devices, shards(): lax.all_to_all(channel_first(second), 'space', split_axis=1, concat_axis=...  204 us
    psum x1, blocking collectives, shards(): lax.psum((masked_sum(first, own_weight), local_count), ('section', 'space'))  64 us
    psum x1, blocking collectives, shards(): lax.psum(masked_squares(first, own_weight, first_mean), ('section', 'spac...  62.5 us
    all_to_all x2, local copies, waits for them, and re-layouts, shards(): lax.all_to_all(channel_first(second), 'space', split_axis=1, concat_axis=...  29.9 us
    reshape x1, local copies, waits for them, and re-layouts, channel_first(): jnp.transpose(values, (0, 3, 1, 2))  27.1 us
    dot_general x1, matrix products, shards(): jnp.einsum('mtpc,cd->mtpd', activation, lax.all_gather(second_weight, 'sp...  11.2 us
    unnamed x15, local copies, waits for them, and re-layouts  10.3 us
    convert_element_type x1, other arithmetic, shards(): output = normalize(moved, second_mean[:, None], second_var[:, None], gain...  9.96 us
  transfers between devices with their start and end apart: 2, of which 1 were waited for; matrix products, arithmetic and copies ran while one was open for 3% of the time, Pallas kernels for 0%

commit v1 on v0

--- a/solution.py
+++ b/solution.py
@@ -38,7 +38,11 @@
     total, count = lax.psum((masked_sum(first, own_weight), local_count), ("section", "space"))
     first_mean = total / count
     first_var = (
-        lax.psum(masked_squares(first, own_weight, first_mean), ("section", "space")) / count
+        jnp.sum(
+            lax.all_gather(masked_squares(first, own_weight, first_mean), ("section", "space")),
+            axis=0,
+        )
+        / count
     )
     activation = normalize(first, first_mean, first_var, first_gain, first_bias).astype(
         jnp.bfloat16

time: 492 us -> 463 us (0.941)
  blocking collectives: 145 us -> 116 us
    psum x1 -> x0, blocking collectives: 62.5 us -> none  [shards(): lax.psum(masked_squares(first, own_weight, first_mean), ('section', 'spac...]
    all_gather x0 -> x1, blocking collectives: none -> 33.3 us  [shards(): lax.all_gather(masked_squares(first, own_weight, first_mean), ('section',...]
where the time goes in v1:
time: 463 us; the launch traced here: 460 us
  waiting for transfers between devices  205 us (44%)
  blocking collectives  116 us (25%)
  local copies, waits for them, and re-layouts  69.3 us (15%)
  other arithmetic  31.6 us (7%)
  matrix products  15.9 us (3%)
  between operations  14.8 us (3%)
  starting transfers between devices  7.81 us (2%)
    all_to_all x1, waiting for transfers between devices, shards(): lax.all_to_all(channel_first(second), 'space', split_axis=1, concat_axis=...  204 us
    psum x1, blocking collectives, shards(): lax.psum((masked_sum(first, own_weight), local_count), ('section', 'space'))  64 us
    all_gather x1, blocking collectives, shards(): lax.all_gather(masked_squares(first, own_weight, first_mean), ('section',...  33.3 us
    all_to_all x2, local copies, waits for them, and re-layouts, shards(): lax.all_to_all(channel_first(second), 'space', split_axis=1, concat_axis=...  29.9 us
    reshape x1, local copies, waits for them, and re-layouts, channel_first(): jnp.transpose(values, (0, 3, 1, 2))  27.1 us
    dot_general x1, matrix products, shards(): jnp.einsum('mtpc,cd->mtpd', activation, lax.all_gather(second_weight, 'sp...  11.2 us
    unnamed x15, local copies, waits for them, and re-layouts  10.3 us
    psum x1, blocking collectives, shards(): lax.psum(jnp.sum(moved * row_weight, axis=(0, 2)), 'section') / count  10.2 us
  transfers between devices with their start and end apart: 2, of which 1 were waited for; matrix products, arithmetic and copies ran while one was open for 3% of the time, Pallas kernels for 0%

profile of v1, /device:TPU:44, one launch (start us, length us, event | category | flops | bytes accessed | tf_op | source)
XLA Modules:
  0.0 460.5 jit_solution(10540511541668194254)
XLA Ops:
  7.2 0.7 all-gather.4.cloned.1.call-update
  8.6 0.7 fusion.12
  9.9 4.7 %multiply_reduce_fusion.1 = (f32[512]{0:T(512)S(1)}, f32[4,784,512]{2,1,0:T(8,128)}) fusion(f32[4]{0:T(128)S(1)} %get-tuple-element.12, bf16[256,512]{1,0:T(8,128)(2,1)} %param.10, bf16[1,4,784,256]{3,2,1,0:T(8,128)(2,1)S(1)} %copy-done), kind=kOutput, calls=%fused_computation.7 | convolution fusion | flops 825294336 | bytes 8292368 | tf_op jit(solution)/shard_map/mtpc,cd->mtpd/dot_general | solution.py:37
  14.6 64.0 %all-reduce = (f32[512]{0:T(512)S(1)}, f32[]{:T(128)}) all-reduce(f32[512]{0:T(512)S(1)} %get-tuple-element.13, f32[]{:T(128)S(6)} %mul.112), channel_id=1, replica_groups=mesh['section'=4,'space'=32] {'section','space'}, use_global_device_ids=true, to_apply=%region_1.0 | all-reduce | flops 513 | bytes 4104 | tf_op jit(solution)/shard_map/psum | solution.py:38
  78.6 0.7 broadcast_divide_fusion.1
  79.3 3.9 fusion.1
  83.2 33.3 %all-gather.1 = f32[128,1,512]{2,1,0:T(1,128)S(1)} all-gather(f32[1,1,512]{2,1,0:T(1,128)S(1)} %bitcast.30), channel_id=2, replica_groups=mesh['section'=4,'space'=32] {'section','space'}, dimensions={0}, use_global_device_ids=true | all-gather | bytes 264192 | tf_op jit(solution)/shard_map/all_gather | solution.py:42
  116.7 1.3 add_rsqrt_fusion
  118.0 11.2 %fusion.2 = f32[4,784,1024]{2,1,0:T(8,128)} fusion(f32[4,784,512]{2,1,0:T(8,128)} %get-tuple-element.14, f32[512]{0:T(512)S(1)} %copy-done.4, f32[512]{0:T(512)S(1)} %get-tuple-element.9, f32[512]{0:T(512)S(1)} %broadcast_divide_fusion.1, f32[512]{0:T(512)S(1)} %copy-done.5, bf16[512,1024]{0,1:T(8,128)(2,1)} %all-gather.4.cloned.1.call-done), kind=kOutput, calls=%fused_computation.8 | convolution fusion | flops 3297968128 | bytes 20324352 | tf_op jit(solution)/shard_map/mtpc,cd->mtpd/dot_general | solution.py:50
  129.3 27.1 %copy.17 = f32[1,1024,3136]{2,0,1:T(1,128)} copy(f32[1,1024,3136]{1,2,0:T(8,128)} %bitcast.29) | data formatting | bytes 25690112 | tf_op jit(solution)/shard_map/reshape | solution.py:24
  156.3 7.8 %all-to-all-start = ((f32[1,1024,3136]{2,0,1:T(1,128)}), f32[1,1024,3136]{2,0,1:T(1,128)}, u32[]{:S(2)}, u32[]{:S(2)}) async-start(f32[1,1024,3136]{2,0,1:T(1,128)} %copy.17), calls=%async_computation | async-start | bytes 26214400 | tf_op jit(solution)/shard_map/all_to_all | solution.py:57
  164.7 0.8 dynamic_slice.11
  165.4 0.8 dynamic_slice.14
  166.2 204.1 %all-to-all-done = f32[1,1024,3136]{2,0,1:T(1,128)} async-done(((f32[1,1024,3136]{2,0,1:T(1,128)}), f32[1,1024,3136]{2,0,1:T(1,128)}, u32[]{:S(2)}, u32[]{:S(2)}) %all-to-all-start) | async-done | bytes 12845088 | tf_op jit(solution)/shard_map/all_to_all | solution.py:57
  370.3 10.3 %copy.19 = f32[1,1024,3136]{2,1,0:T(8,128)} copy(f32[1,1024,3136]{2,0,1:T(1,128)} %all-to-all-done) | data formatting | bytes 25690112
  380.6 17.0 %copy.18 = f32[1,32,32,3136]{3,2,1,0:T(8,128)} copy(f32[1,32,32,3136]{3,1,2,0:T(8,128)} %bitcast.26) | data formatting | bytes 25690112 | tf_op jit(solution)/shard_map/all_to_all | solution.py:57
  397.6 5.7 %multiply_reduce_fusion = f32[32]{0:T(128)S(1)} fusion(f32[1,32,32,3136]{3,1,2,0:T(8,128)} %bitcast.27, f32[32,3136]{1,0:T(8,128)S(1)} %broadcast_in_dim.5), kind=kLoop, calls=%fused_computation.2 | loop fusion | flops 6422496 | bytes 13246592 | tf_op jit(solution)/shard_map/reduce_sum | solution.py:59
  403.3 10.2 %psum.30 = f32[32]{0:T(128)S(1)} all-reduce(f32[32]{0:T(128)S(1)} %multiply_reduce_fusion), channel_id=1, replica_groups=mesh['section'=4,'space'=32] {'section'}, use_global_device_ids=true, to_apply=%region_7.0 | all-reduce | flops 32 | bytes 256 | tf_op jit(solution)/shard_map/psum | solution.py:59
  413.4 0.7 broadcast_divide_fusion.3
  414.2 6.6 %fusion = f32[32]{0:T(128)S(1)} fusion(f32[1,32,32,3136]{3,1,2,0:T(8,128)} %bitcast.28, f32[32]{0:T(128)S(1)} %broadcast_divide_fusion.3, f32[32,3136]{1,0:T(8,128)S(1)} %broadcast_in_dim.5), kind=kLoop, calls=%fused_computation.1 | loop fusion | flops 12845024 | bytes 13246720 | tf_op jit(solution)/shard_map/reduce_sum | solution.py:61
  420.8 8.8 %psum.31 = f32[32]{0:T(128)S(1)} all-reduce(f32[32]{0:T(128)S(1)} %fusion), channel_id=1, replica_groups=mesh['section'=4,'space'=32] {'section'}, use_global_device_ids=true, to_apply=%region_9.0 | all-reduce | flops 32 | bytes 256 | tf_op jit(solution)/shard_map/psum | solution.py:61
  429.5 1.2 add_rsqrt_fusion.1
  430.8 12.9 %all_to_all.16 = f32[1,32,100352]{2,1,0:T(8,128)} reshape(f32[1,32,32,3136]{3,2,1,0:T(8,128)} %copy.18) | data formatting | bytes 25690112 | tf_op jit(solution)/shard_map/all_to_all | solution.py:57
  443.7 10.0 %maximum_convert_fusion = bf16[1,32,100352]{2,1,0:T(8,128)(2,1)} fusion(f32[1,32,100352]{2,1,0:T(8,128)} %all_to_all.16, f32[32]{0:T(128)S(1)} %dynamic_slice.14, f32[32]{0:T(128)S(1)} %get-tuple-element.7, f32[32]{0:T(128)S(1)} %broadcast_divide_fusion.3, f32[32]{0:T(128)S(1)} %dynamic_slice.11), kind=kLoop, calls=%fused_computation.3 | loop fusion | flops 19267584 | bytes 19268096 | tf_op jit(solution)/shard_map/convert_element_type | solution.py:66
  (22 shorter events, 1.5 us)
Async XLA Ops:
  7.2 2.7 copy-start
  7.2 110.8 %all-gather.4.cloned.1.call-start = ((), (), s32[]{:S(2)}) async-start(), calls=%async_computation.1 | async-start | bytes 1081344 | tf_op jit(solution)/shard_map/all_gather | solution.py:53
  14.6 103.4 %copy-start.4 = (f32[512]{0:T(512)S(1)}, f32[512]{0:T(512)}, u32[]{:S(2)}) copy-start(f32[512]{0:T(512)} %param.12) | copy-start | bytes 6148
  14.6 103.4 %copy-start.5 = (f32[512]{0:T(512)S(1)}, f32[512]{0:T(512)}, u32[]{:S(2)}) copy-start(f32[512]{0:T(512)} %param.11) | copy-start | bytes 6148
  79.3 50.0 %copy-start.2 = (f32[512]{0:T(512)}, f32[512]{0:T(512)S(1)}, u32[]{:S(2)}) copy-start(f32[512]{0:T(512)S(1)} %broadcast_divide_fusion.1) | copy-start | bytes 6148
  156.3 7.8 %copy-start.6 = (s32[1,128]{1,0:T(1,128)S(1)}, s32[1,128]{1,0:T(1,128)}, u32[]{:S(2)}) copy-start(s32[1,128]{1,0:T(1,128)} %param.9) | copy-start | bytes 1540
  156.3 214.0 %all-to-all-start = ((f32[1,1024,3136]{2,0,1:T(1,128)}), f32[1,1024,3136]{2,0,1:T(1,128)}, u32[]{:S(2)}, u32[]{:S(2)}) async-start(f32[1,1024,3136]{2,0,1:T(1,128)} %copy.17), calls=%async_computation | async-start | bytes 26214400 | tf_op jit(solution)/shard_map/all_to_all | solution.py:57
  414.1 29.5 %copy-start.3 = (f32[32]{0:T(128)}, f32[32]{0:T(128)S(1)}, u32[]{:S(2)}) copy-start(f32[32]{0:T(128)S(1)} %broadcast_divide_fusion.3) | copy-start | bytes 388
  443.6 10.0 %copy-start.1 = (bf16[1,4,784,256]{3,2,1,0:T(8,128)(2,1)S(1)}, bf16[1,4,784,256]{3,2,1,0:T(8,128)(2,1)}, u32[]{:S(2)}) copy-start(bf16[1,4,784,256]{3,2,1,0:T(8,128)(2,1)} %param.8) | copy-start | bytes 4816900
Sparse Core Ops, SparseCore 0:
  10.3 42.4 all-gather.3
